TPU v7x, 512 devices: a whole 4x8x8 slice. The times are simulated.
512 devices in a mesh: dp: 32 (over x, y), segment: 2 (over core), mp: 8 (over z).
Axes of the slice: x: 4, y: 8, z: 8, core: 2. Of those that a mesh axis runs over, the one named last changes fastest.
Arguments:
- frames: bfloat16 [2, 8192, 1280], P(None, ('dp', 'mp')), may hold values from -8 to 8
- dec_states: bfloat16 [2, 2048, 1280], P(None, 'dp'), may hold values from -8 to 8
- out_grad: bfloat16 [2, 2048, 1280], P(None, 'dp'), may hold values from -3 to 3
- frame_lengths: int32 [2, 32, 4], P(None, 'dp'), may hold values from 1 to 128, 256 in all within a row
- token_lengths: int32 [2, 32, 4], P(None, 'dp'), may hold values from 1 to 32, 64 in all within a row
- weights: bfloat16 [2, 4, 1024, 1280], P('segment', None, 'mp'), may hold values from -1 to 1
- norm_gains: float32 [3, 1280], replicated, may hold values from 0.25 to 1.75
- norm_biases: float32 [3, 1280], replicated, may hold values from -2 to 2
Outputs:
- gradient: float32 [2, 3, 1024, 1280], P('segment', None, 'mp')
Inputs may be any that keep to these rules, and one draw needn't show every extreme that they name: `frame_lengths`: the 4 utterance lengths of each micro-batch and group sum to 256. `token_lengths`: the 4 token counts of each micro-batch and group sum to 64.
All inputs are finite; a program needn't handle non-finite values.
Results may differ from a plain program's by a relative error of at most 0.04.
Values may be sent and summed in bfloat16 or wider, within the bound.
No kernel may reach another device: no remote copies, remote signals or barrier semaphores. Data moves between devices by JAX's collectives and lax.ppermute only.
A program may use at most 64 MiB of HBM per device.

v0:
```python
import math
import jax
import jax.numpy as jnp
from jax import lax
from jax.sharding import PartitionSpec as P

HS = 64
EPSILON = 1e-05
ROWS_DIMS = (((0,), (0,)), ((), ()))
FEAT_DIMS = (((1,), (1,)), ((), ()))


def layer_norm(values, norm_gain, offset):
    center = values - jnp.mean(values, axis=-1, keepdims=True)
    variance = jnp.mean(center * center, axis=-1, keepdims=True)
    return center * lax.rsqrt(variance + EPSILON) * norm_gain + offset


def norm_backward(grad_out, values, norm_gain):
    center = values - jnp.mean(values, axis=-1, keepdims=True)
    variance = jnp.mean(center * center, axis=-1, keepdims=True)
    inverse = lax.rsqrt(variance + EPSILON)
    normed = center * inverse
    scaled = grad_out * norm_gain
    return inverse * (
        scaled
        - jnp.mean(scaled, axis=-1, keepdims=True)
        - normed * jnp.mean(scaled * normed, axis=-1, keepdims=True)
    )


def utterance_ids(lengths, row_count):
    bounds = jnp.cumsum(lengths, dtype=jnp.int32)
    places = jnp.arange(row_count, dtype=jnp.int32)
    return jnp.sum((places[:, None] >= bounds[None, :]).astype(jnp.int32), axis=1)


def project(row_block, matrix):
    return lax.dot_general(row_block, matrix, FEAT_DIMS, preferred_element_type=jnp.float32).astype(
        jnp.bfloat16
    )


def outer_rows(left_rows, right_rows):
    return lax.dot_general(left_rows, right_rows, ROWS_DIMS, preferred_element_type=jnp.float32)


def split_heads(row_block):
    return row_block.reshape(row_block.shape[0], -1, HS)


def attend(queries, key_rows, value_rows, allowed):
    scaling = 1.0 / math.sqrt(HS)
    scores = (
        jnp.einsum(
            "qhd,khd->hqk",
            split_heads(queries),
            split_heads(key_rows),
            preferred_element_type=jnp.float32,
        )
        * scaling
    )
    scores = jnp.where(allowed[None], scores, -1e30)
    highest = jnp.max(scores, axis=-1, keepdims=True)
    raised = jnp.exp(scores - highest)
    attn_probs = raised / jnp.sum(raised, axis=-1, keepdims=True)
    context = jnp.einsum(
        "hqk,khd->qhd",
        attn_probs.astype(jnp.bfloat16),
        split_heads(value_rows),
        preferred_element_type=jnp.float32,
    )
    return (context.reshape(queries.shape[0], -1).astype(jnp.bfloat16), attn_probs)


def attend_backward(queries, key_rows, value_rows, attn_probs, grad_context):
    scaling = 1.0 / math.sqrt(HS)
    grad_heads = split_heads(grad_context)
    grad_probs = jnp.einsum(
        "qhd,khd->hqk", grad_heads, split_heads(value_rows), preferred_element_type=jnp.float32
    )
    grad_scores = (
        attn_probs * (grad_probs - jnp.sum(grad_probs * attn_probs, axis=-1, keepdims=True))
    ).astype(jnp.bfloat16)
    key_grad = (
        jnp.einsum(
            "hqk,qhd->khd", grad_scores, split_heads(queries), preferred_element_type=jnp.float32
        )
        * scaling
    )
    key_grad = key_grad.reshape(key_rows.shape[0], -1).astype(jnp.bfloat16)
    value_grad = jnp.einsum(
        "hqk,qhd->khd",
        attn_probs.astype(jnp.bfloat16),
        grad_heads,
        preferred_element_type=jnp.float32,
    )
    value_grad = value_grad.reshape(key_rows.shape[0], -1).astype(jnp.bfloat16)
    return (key_grad, value_grad)


def spread(block, axis):
    size = lax.axis_size(axis)
    return lax.all_to_all(jnp.broadcast_to(block[None], (size,) + block.shape), axis, 0, 0)


def share_sum(blocks, axis):
    return jnp.sum(lax.all_to_all(blocks, axis, 0, 0).astype(jnp.float32), axis=0)


def swap(block):
    return lax.ppermute(block, "segment", [(0, 1), (1, 0)])


def to_chunks(block, parts):
    high, wide = (block.shape[0] // 8, block.shape[1] // 128)
    tiles = block.reshape(high, 8, wide, 128).transpose(0, 2, 1, 3).reshape(-1, 8, 128)
    each = -(-tiles.shape[0] // parts)
    tiles = jnp.pad(tiles, ((0, each * parts - tiles.shape[0]), (0, 0), (0, 0)))
    return tiles.reshape(parts, each, 8, 128)


def from_chunks(chunks, rows, cols):
    high, wide = (rows // 8, cols // 128)
    tiles = chunks.reshape(-1, 8, 128)[: high * wide]
    return tiles.reshape(high, wide, 8, 128).transpose(0, 2, 1, 3).reshape(rows, cols)


def shards(
    frames, dec_states, out_grad, frame_lengths, token_lengths, weights, norm_gains, norm_biases
):
    core = lax.axis_index("segment")
    first = core == 0
    own = weights[0]
    shard_rows, features = frames.shape[1:]
    mp = lax.axis_size("mp")
    dp = lax.axis_size("dp")
    head_cols = own.shape[1]
    rows = shard_rows * mp
    half = features // 2

    def mine(array):
        return lax.dynamic_index_in_dim(array, core, 0, keepdims=False)

    inputs = mine(frames)
    tokens = mine(dec_states)
    upstream = mine(out_grad)
    frame_ids = utterance_ids(mine(frame_lengths)[0], rows)
    token_ids = utterance_ids(mine(token_lengths)[0], tokens.shape[0])
    out_sent = lax.ppermute(own[3, :, half:], "segment", [(0, 1)])
    out_part = jnp.where(first, own[3, :, :half], out_sent)
    out_part = lax.all_gather(out_part, "mp", axis=0, tiled=True)
    out_rest = swap(out_part)
    enc_full = spread(inputs, "mp").reshape(rows, features)
    other = swap(own)
    enc = jnp.where(first, own, other)
    dec = jnp.where(first, other, own)
    normed = layer_norm(enc_full.astype(jnp.float32), norm_gains[0], norm_biases[0]).astype(
        jnp.bfloat16
    )
    queries = project(normed, enc[0])
    key_rows = project(normed, enc[1])
    value_rows = project(normed, enc[2])
    context, probs = attend(queries, key_rows, value_rows, frame_ids[:, None] == frame_ids[None, :])
    context_full = spread(context, "mp").transpose(1, 0, 2).reshape(rows, mp * head_cols)
    out_mine = jnp.dot(context_full, out_part, preferred_element_type=jnp.float32)
    out_other = jnp.dot(context_full, out_rest, preferred_element_type=jnp.float32)
    summed = jnp.concatenate(
        [jnp.where(first, out_mine, out_other), jnp.where(first, out_other, out_mine)], axis=1
    )
    states_full = (enc_full.astype(jnp.float32) + summed).astype(jnp.bfloat16)
    states = lax.dynamic_slice_in_dim(states_full, lax.axis_index("mp") * shard_rows, shard_rows, 0)
    state_normed = layer_norm(
        states_full.astype(jnp.float32), norm_gains[2], norm_biases[2]
    ).astype(jnp.bfloat16)
    token_normed = layer_norm(tokens.astype(jnp.float32), norm_gains[1], norm_biases[1]).astype(
        jnp.bfloat16
    )
    dec_queries = project(token_normed, dec[0])
    dec_keys = project(state_normed, dec[1])
    dec_values = project(state_normed, dec[2])
    dec_context, dec_probs = attend(
        dec_queries, dec_keys, dec_values, token_ids[:, None] == frame_ids[None, :]
    )
    grad_context = project(upstream, dec[3])
    dec_key_grad, dec_value_grad = attend_backward(
        dec_queries, dec_keys, dec_values, dec_probs, grad_context
    )
    partial = (
        jnp.dot(dec_key_grad, dec[1], preferred_element_type=jnp.float32)
        + jnp.dot(dec_value_grad, dec[2], preferred_element_type=jnp.float32)
    ).astype(jnp.bfloat16)

    def combine(term):
        left, right = (term[:, :half], term[:, half:])
        sent = swap(jnp.where(first, right, left).astype(jnp.bfloat16))
        return (jnp.where(first, left, right) + sent.astype(jnp.float32)).astype(jnp.bfloat16)

    def reduce_groups(term):
        total = share_sum(to_chunks(term, dp), "dp").astype(jnp.bfloat16)
        return from_chunks(spread(total, "dp"), 3 * head_cols, half)

    dec_term = jnp.concatenate(
        [
            outer_rows(dec_key_grad, state_normed),
            outer_rows(dec_value_grad, state_normed),
            outer_rows(dec_context, upstream),
        ]
    )
    pieces = lax.all_to_all(partial.reshape(mp, shard_rows, features), "mp", 0, 0)
    pieces, dec_part = lax.optimization_barrier((pieces, combine(dec_term)))
    dec_total = lax.psum(dec_part, "dp")
    summed = jnp.sum(pieces.astype(jnp.float32), axis=0)
    grads = norm_backward(summed, states.astype(jnp.float32), norm_gains[2]).astype(jnp.bfloat16)
    grads_full = spread(grads, "mp").reshape(rows, features)
    att_grad = project(grads_full, enc[3])
    enc_key_grad, enc_value_grad = attend_backward(queries, key_rows, value_rows, probs, att_grad)
    enc_term = jnp.concatenate(
        [
            outer_rows(enc_key_grad, normed),
            outer_rows(enc_value_grad, normed),
            outer_rows(context, grads_full),
        ]
    )
    enc_total = reduce_groups(combine(enc_term))
    kept = jnp.where(first, enc_total, dec_total)
    got = swap(jnp.where(first, dec_total, enc_total))
    gradient = jnp.concatenate(
        [jnp.where(first, kept, got), jnp.where(first, got, kept)], axis=1
    ).astype(jnp.float32)
    return gradient.reshape(1, 3, head_cols, features)


def solution(mesh):
    placed = (
        P(None, ("dp", "mp"), None),
        P(None, "dp", None),
        P(None, "dp", None),
        P(None, "dp", None),
        P(None, "dp", None),
        P("segment", None, "mp", None),
        P(),
        P(),
    )
    return jax.shard_map(
        shards,
        mesh=mesh,
        in_specs=placed,
        out_specs=P("segment", None, "mp", None),
        check_vma=False,
    )
```

profile of v0, /device:TPU:1, one launch (start us, length us, event | category | flops | bytes accessed | tf_op | source)
XLA Modules:
  0.0 379.2 jit_solution(9192799755561751875)
XLA Ops:
  8.5 10.9 %all-to-all-start = ((bf16[8,32,1280]{2,1,0:T(8,128)(2,1)}), bf16[8,32,1280]{2,1,0:T(8,128)(2,1)S(1)}, u32[]{:S(2)}, u32[]{:S(2)}) async-start(bf16[8,32,1280]{2,1,0:T(8,128)(2,1)} %broadcast_in_dim.31), calls=%async_computation | async-start | bytes 1310720 | tf_op jit(solution)/shard_map/all_to_all | solution.py:104
  19.4 2.9 collective-permute-start
  27.3 12.8 %all-to-all-done = bf16[8,32,1280]{2,1,0:T(8,128)(2,1)S(1)} async-done(((bf16[8,32,1280]{2,1,0:T(8,128)(2,1)}), bf16[8,32,1280]{2,1,0:T(8,128)(2,1)S(1)}, u32[]{:S(2)}, u32[]{:S(2)}) %all-to-all-start) | async-done | bytes 655392 | tf_op jit(solution)/shard_map/all_to_all | solution.py:104
  41.4 1.5 broadcast_select_fusion.1
  44.4 23.2 %all-gather.2.cloned.1.call-done = bf16[1024,640]{1,0:T(8,128)(2,1)} async-done(((bf16[128,640]{1,0:T(8,128)(2,1)}), bf16[1024,640]{1,0:T(8,128)(2,1)}) %all-gather.2.cloned.1.call-update) | async-done | bytes 1310736 | tf_op jit(solution)/shard_map/all_gather | solution.py:152
  67.6 7.2 %collective-permute-start.2 = (bf16[1024,640]{1,0:T(8,128)(2,1)}, bf16[1024,640]{1,0:T(8,128)(2,1)}, u32[]{:S(2)}, u32[]{:S(2)}) collective-permute-start(bf16[1024,640]{1,0:T(8,128)(2,1)} %all-gather.2.cloned.1.call-done), channel_id=1, source_target_pairs={{0,8},{8,0},{1,9},{9,1},{2,10},{10,2},{3,11},{11,3},{4,12},{12,4},... | collective-permute-start | bytes 3932168 | tf_op jit(solution)/shard_map/ppermute | solution.py:112
  77.4 3.9 %all-to-all-start.1 = ((bf16[8,256,128]{1,2,0:T(8,128)(2,1)}), bf16[8,256,128]{1,2,0:T(8,128)(2,1)S(1)}, u32[]{:S(2)}, u32[]{:S(2)}) async-start(bf16[8,256,128]{1,2,0:T(8,128)(2,1)} %broadcast_in_dim.34), calls=%async_computation.1 | async-start | bytes 1048576 | tf_op jit(solution)/shard_map/all_to_all | solution.py:104
  83.4 1.4 copy.34
  85.7 1.4 copy.35
  87.1 12.2 %all-to-all-done.1 = bf16[8,256,128]{1,2,0:T(8,128)(2,1)S(1)} async-done(((bf16[8,256,128]{1,2,0:T(8,128)(2,1)}), bf16[8,256,128]{1,2,0:T(8,128)(2,1)S(1)}, u32[]{:S(2)}, u32[]{:S(2)}) %all-to-all-start.1) | async-done | bytes 524320 | tf_op jit(solution)/shard_map/all_to_all | solution.py:104
  99.3 1.9 fusion.72
  101.2 1.9 broadcast_select_fusion.7
  107.3 2.4 fusion.25
  111.0 1.3 fusion.17
  114.6 2.2 fusion.2
  116.8 3.5 all-to-all-start.2
  120.3 1.6 pad_maximum_fusion
  122.0 2.4 collective-permute-start.3
  126.9 14.1 %all-to-all-done.2 = bf16[8,32,1280]{2,1,0:T(8,128)(2,1)S(1)} async-done(((bf16[8,32,1280]{2,1,0:T(8,128)(2,1)}), bf16[8,32,1280]{2,1,0:T(8,128)(2,1)S(1)}, u32[]{:S(2)}, u32[]{:S(2)}) %all-to-all-start.2) | async-done | bytes 655392 | tf_op jit(solution)/shard_map/all_to_all | solution.py:210
  141.5 22.3 %all_to_all.30 = bf16[8,32,1280]{2,1,0:T(8,128)(2,1)S(1)} all-to-all(bf16[8,32,1280]{2,1,0:T(8,128)(2,1)S(1)} %broadcast_in_dim.37), channel_id=1, replica_groups=mesh['dp'=32,'segment'=2,'mp'=8] {'mp'}, dimensions={0} | all-to-all | bytes 1310720 | tf_op jit(solution)/shard_map/all_to_all | solution.py:104
  163.8 1.4 convolution_convert_fusion
  165.5 1.5 convolution_convert_fusion.7
  167.3 1.4 fusion.16
  169.5 3.2 collective-permute-start.4
  172.7 1.5 collective-permute-done.4
  174.4 23.2 %all_to_all.31 = bf16[32,8,8,128]{3,2,1,0:T(8,128)(2,1)S(1)} all-to-all(bf16[32,8,8,128]{3,2,1,0:T(8,128)(2,1)S(1)} %bitcast.176), channel_id=1, replica_groups=mesh['dp'=32,'segment'=2,'mp'=8] {'dp'}, dimensions={0} | all-to-all | bytes 1048576 | tf_op jit(solution)/shard_map/all_to_all | solution.py:108
  198.6 8.1 %all-to-all-start.5 = ((bf16[32,8,8,128]{3,2,1,0:T(8,128)(2,1)}), bf16[32,8,8,128]{3,2,1,0:T(8,128)(2,1)S(1)}, u32[]{:S(2)}, u32[]{:S(2)}) async-start(bf16[32,8,8,128]{3,2,1,0:T(8,128)(2,1)} %broadcast_in_dim.42), calls=%async_computation.5 | async-start | bytes 1048576 | tf_op jit(solution)/shard_map/all_to_all | solution.py:104
  207.5 13.3 %all-to-all-done.5 = bf16[32,8,8,128]{3,2,1,0:T(8,128)(2,1)S(1)} async-done(((bf16[32,8,8,128]{3,2,1,0:T(8,128)(2,1)}), bf16[32,8,8,128]{3,2,1,0:T(8,128)(2,1)S(1)}, u32[]{:S(2)}, u32[]{:S(2)}) %all-to-all-start.5) | async-done | bytes 524320 | tf_op jit(solution)/shard_map/all_to_all | solution.py:104
  220.8 140.2 %all-reduce.3.cloned.1.call-done = bf16[384,640]{1,0:T(8,128)(2,1)} async-done(((bf16[384,640]{1,0:T(8,128)(2,1)}), bf16[384,640]{1,0:T(8,128)(2,1)}) %all-reduce.3.cloned.1.call-update) | async-done | bytes 491536 | tf_op jit(solution)/shard_map/psum | solution.py:212
  361.1 8.2 %collective-permute-start.5 = (bf16[384,640]{1,0:T(8,128)(2,1)S(1)}, bf16[384,640]{1,0:T(8,128)(2,1)S(1)}, u32[]{:S(2)}, u32[]{:S(2)}) collective-permute-start(bf16[384,640]{1,0:T(8,128)(2,1)S(1)} %broadcast_select_fusion.4), channel_id=1, source_target_pairs={{0,8},{8,0},{1,9},{9,1},{2,10},{10,2},{3,11},{11,3},{4,12},{12,4},... | collective-permute-start | bytes 1474568 | tf_op jit(solution)/shard_map/ppermute | solution.py:112
  369.3 1.5 collective-permute-done.5
  370.9 1.4 maximum_convert_fusion
  (142 shorter events, 29.2 us)
Async XLA Ops:
  6.5 78.3 %copy-start = (bf16[2,64,1280]{2,1,0:T(8,128)(2,1)S(1)}, bf16[2,64,1280]{2,1,0:T(8,128)(2,1)}, u32[]{:S(2)}) copy-start(bf16[2,64,1280]{2,1,0:T(8,128)(2,1)} %param.10) | copy-start | bytes 983044
  6.5 12.9 %copy-start.4 = (bf16[1,4,128,1280]{3,2,1,0:T(8,128)(2,1)S(1)}, bf16[1,4,128,1280]{3,2,1,0:T(8,128)(2,1)}, u32[]{:S(2)}) copy-start(bf16[1,4,128,1280]{3,2,1,0:T(8,128)(2,1)} %param.13) | copy-start | bytes 3932164
  6.5 17.1 %copy-start.20 = (s32[2,1,4]{2,1,0:T(1,128)S(1)}, s32[2,1,4]{2,1,0:T(1,128)}, u32[]{:S(2)}) copy-start(s32[2,1,4]{2,1,0:T(1,128)} %param.11) | copy-start | bytes 100
  6.5 17.1 %copy-start.21 = (s32[2,1,4]{2,1,0:T(1,128)S(1)}, s32[2,1,4]{2,1,0:T(1,128)}, u32[]{:S(2)}) copy-start(s32[2,1,4]{2,1,0:T(1,128)} %param.12) | copy-start | bytes 100
  6.5 17.4 %copy-start.8 = (bf16[2,64,1280]{2,1,0:T(8,128)(2,1)S(1)}, bf16[2,64,1280]{2,1,0:T(8,128)(2,1)}, u32[]{:S(2)}) copy-start(bf16[2,64,1280]{2,1,0:T(8,128)(2,1)} %param.9) | copy-start | bytes 983044
  7.6 18.3 %copy-start.14 = (f32[3,1280]{1,0:T(4,128)S(1)}, f32[3,1280]{1,0:T(4,128)}, u32[]{:S(2)}) copy-start(f32[3,1280]{1,0:T(4,128)} %param.15) | copy-start | bytes 46084
  7.6 18.3 %copy-start.15 = (f32[3,1280]{1,0:T(4,128)S(1)}, f32[3,1280]{1,0:T(4,128)}, u32[]{:S(2)}) copy-start(f32[3,1280]{1,0:T(4,128)} %param.14) | copy-start | bytes 46084
  8.5 31.6 %all-to-all-start = ((bf16[8,32,1280]{2,1,0:T(8,128)(2,1)}), bf16[8,32,1280]{2,1,0:T(8,128)(2,1)S(1)}, u32[]{:S(2)}, u32[]{:S(2)}) async-start(bf16[8,32,1280]{2,1,0:T(8,128)(2,1)} %broadcast_in_dim.31), calls=%async_computation | async-start | bytes 1310720 | tf_op jit(solution)/shard_map/all_to_all | solution.py:104
  19.3 48.2 %all-gather.2.cloned.1.call-start = ((), (), s32[]{:S(2)}) async-start(), calls=%async_computation.6 | async-start | bytes 1474560 | tf_op jit(solution)/shard_map/all_gather | solution.py:152
  19.4 21.6 %collective-permute-start = (bf16[4,128,1280]{2,1,0:T(8,128)(2,1)S(1)}, bf16[4,128,1280]{2,1,0:T(8,128)(2,1)}, u32[]{:S(2)}, u32[]{:S(2)}) collective-permute-start(bf16[4,128,1280]{2,1,0:T(8,128)(2,1)S(1)} %bitcast.177), channel_id=1, source_target_pairs={{0,8},{8,0},{1,9},{9,1},{2,10},{10,2},{3,11},{11,3},{4,12},{12,4},... | collective-permute-start | bytes 3932168 | tf_op jit(solution)/shard_map/ppermute | solution.py:112
  22.3 4.3 %collective-permute-start.1 = (bf16[128,640]{1,0:T(8,128)(2,1)S(1)}, bf16[128,640]{1,0:T(8,128)(2,1)S(1)}, u32[]{:S(2)}, u32[]{:S(2)}) collective-permute-start(bf16[128,640]{1,0:T(8,128)(2,1)S(1)} %slice_bitcast_fusion.18), channel_id=1, source_target_pairs={{0,8},{1,9},{2,10},{3,11},{4,12},{5,13},{6,14},{7,15},{16,24},{17,... | collective-permute-start | bytes 491528 | tf_op jit(solution)/shard_map/ppermute | solution.py:150
  24.0 1.9 copy-start.18
  25.3 50.7 %copy-start.10 = (pred[256,256]{0,1:T(8,128)(4,1)}, pred[256,256]{0,1:T(8,128)(4,1)S(1)}, u32[]{:S(2)}) copy-start(pred[256,256]{0,1:T(8,128)(4,1)S(1)} %broadcast_compare_fusion) | copy-start | bytes 196612
  42.9 41.9 %copy-start.2 = (bf16[4,128,1280]{2,1,0:T(8,128)(2,1)}, bf16[4,128,1280]{2,1,0:T(8,128)(2,1)S(1)}, u32[]{:S(2)}) copy-start(bf16[4,128,1280]{2,1,0:T(8,128)(2,1)S(1)} %get-tuple-element.22) | copy-start | bytes 3932164
  43.3 32.7 %copy-start.22 = (bf16[256,128]{0,1:T(8,128)(2,1)}, bf16[256,128]{0,1:T(8,128)(2,1)S(1)}, u32[]{:S(2)}) copy-start(bf16[256,128]{0,1:T(8,128)(2,1)S(1)} %convolution_convert_fusion.5) | copy-start | bytes 196612
  44.0 32.5 %copy-start.24 = (bf16[256,128]{0,1:T(8,128)(2,1)}, bf16[256,128]{0,1:T(8,128)(2,1)S(1)}, u32[]{:S(2)}) copy-start(bf16[256,128]{0,1:T(8,128)(2,1)S(1)} %convolution_convert_fusion.6) | copy-start | bytes 196612
  44.3 32.2 %copy-start.26 = (bf16[256,128]{0,1:T(8,128)(2,1)}, bf16[256,128]{0,1:T(8,128)(2,1)S(1)}, u32[]{:S(2)}) copy-start(bf16[256,128]{0,1:T(8,128)(2,1)S(1)} %convolution_convert_fusion.4) | copy-start | bytes 196612
  67.6 31.7 %collective-permute-start.2 = (bf16[1024,640]{1,0:T(8,128)(2,1)}, bf16[1024,640]{1,0:T(8,128)(2,1)}, u32[]{:S(2)}, u32[]{:S(2)}) collective-permute-start(bf16[1024,640]{1,0:T(8,128)(2,1)} %all-gather.2.cloned.1.call-done), channel_id=1, source_target_pairs={{0,8},{8,0},{1,9},{9,1},{2,10},{10,2},{3,11},{11,3},{4,12},{12,4},... | collective-permute-start | bytes 3932168 | tf_op jit(solution)/shard_map/ppermute | solution.py:112
  77.4 21.9 %all-to-all-start.1 = ((bf16[8,256,128]{1,2,0:T(8,128)(2,1)}), bf16[8,256,128]{1,2,0:T(8,128)(2,1)S(1)}, u32[]{:S(2)}, u32[]{:S(2)}) async-start(bf16[8,256,128]{1,2,0:T(8,128)(2,1)} %broadcast_in_dim.34), calls=%async_computation.1 | async-start | bytes 1048576 | tf_op jit(solution)/shard_map/all_to_all | solution.py:104
  104.0 1.7 copy-start.12
  112.4 2.2 copy-start.1
  116.8 24.2 %all-to-all-start.2 = ((bf16[8,32,1280]{2,1,0:T(8,128)(2,1)}), bf16[8,32,1280]{2,1,0:T(8,128)(2,1)S(1)}, u32[]{:S(2)}, u32[]{:S(2)}) async-start(bf16[8,32,1280]{2,1,0:T(8,128)(2,1)} %bitcast.37), calls=%async_computation.2 | async-start | bytes 1310720 | tf_op jit(solution)/shard_map/all_to_all | solution.py:210
  122.0 3.9 %collective-permute-start.3 = (bf16[384,640]{1,0:T(8,128)(2,1)S(1)}, bf16[384,640]{1,0:T(8,128)(2,1)S(1)}, u32[]{:S(2)}, u32[]{:S(2)}) collective-permute-start(bf16[384,640]{1,0:T(8,128)(2,1)S(1)} %select_convert_fusion.1), channel_id=1, source_target_pairs={{0,8},{8,0},{1,9},{9,1},{2,10},{10,2},{3,11},{11,3},{4,12},{12,4},... | collective-permute-start | bytes 1474568 | tf_op jit(solution)/shard_map/ppermute | solution.py:112
  163.8 1.7 copy-start.23
  163.8 1.7 copy-start.25
  163.8 1.7 copy-start.31
  165.4 1.5 copy-start.27
  169.5 4.7 %collective-permute-start.4 = (bf16[384,640]{1,0:T(8,128)(2,1)S(1)}, bf16[384,640]{1,0:T(8,128)(2,1)S(1)}, u32[]{:S(2)}, u32[]{:S(2)}) collective-permute-start(bf16[384,640]{1,0:T(8,128)(2,1)S(1)} %select_convert_fusion), channel_id=1, source_target_pairs={{0,8},{8,0},{1,9},{9,1},{2,10},{10,2},{3,11},{11,3},{4,12},{12,4},... | collective-permute-start | bytes 1474568 | tf_op jit(solution)/shard_map/ppermute | solution.py:112
  198.6 22.2 %all-to-all-start.5 = ((bf16[32,8,8,128]{3,2,1,0:T(8,128)(2,1)}), bf16[32,8,8,128]{3,2,1,0:T(8,128)(2,1)S(1)}, u32[]{:S(2)}, u32[]{:S(2)}) async-start(bf16[32,8,8,128]{3,2,1,0:T(8,128)(2,1)} %broadcast_in_dim.42), calls=%async_computation.5 | async-start | bytes 1048576 | tf_op jit(solution)/shard_map/all_to_all | solution.py:104
  206.7 154.3 %all-reduce.3.cloned.1.call-start = ((), (), s32[]{:S(2)}) async-start(), calls=%async_computation.7 | async-start | bytes 983040 | tf_op jit(solution)/shard_map/psum | solution.py:212
  361.0 9.8 %copy-start.6 = (bf16[384,640]{1,0:T(8,128)(2,1)S(1)}, bf16[384,640]{1,0:T(8,128)(2,1)}, u32[]{:S(2)}) copy-start(bf16[384,640]{1,0:T(8,128)(2,1)} %all-reduce.3.cloned.1.call-done) | copy-start | bytes 1474564
  361.1 9.7 %collective-permute-start.5 = (bf16[384,640]{1,0:T(8,128)(2,1)S(1)}, bf16[384,640]{1,0:T(8,128)(2,1)S(1)}, u32[]{:S(2)}, u32[]{:S(2)}) collective-permute-start(bf16[384,640]{1,0:T(8,128)(2,1)S(1)} %broadcast_select_fusion.4), channel_id=1, source_target_pairs={{0,8},{8,0},{1,9},{9,1},{2,10},{10,2},{3,11},{11,3},{4,12},{12,4},... | collective-permute-start | bytes 1474568 | tf_op jit(solution)/shard_map/ppermute | solution.py:112
  (12 other events, 15.6 us)
Sparse Core Ops, SparseCore 0:
  27.4 40.0 all-gather.1
  210.9 150.0 all-reduce.2
where the time goes:
time: 380 us; the launch traced here: 379 us
  waiting for transfers between devices  220 us (58%)
  starting transfers between devices  51.7 us (14%)
  blocking collectives  45.5 us (12%)
  matrix products  25.7 us (7%)
  between operations  14 us (4%)
  other arithmetic  13.8 us (4%)
  local copies, waits for them, and re-layouts  8.81 us (2%)
    psum x1, waiting for transfers between devices, shards(): dec_total = lax.psum(dec_part, 'dp')  140 us
    all_to_all x3, waiting for transfers between devices, spread(): lax.all_to_all(jnp.broadcast_to(block[None], (size,) + block.shape), axis...  38.3 us
    ppermute x5, starting transfers between devices, swap(): return lax.ppermute(block, 'segment', [(0, 1), (1, 0)])  23.9 us
    all_to_all x1, blocking collectives, share_sum(): lax.all_to_all(blocks, axis, 0, 0).astype(jnp.float32)  23.2 us
    all_gather x1, waiting for transfers between devices, shards(): out_part = lax.all_gather(out_part, 'mp', axis=0, tiled=True)  23.2 us
    all_to_all x3, starting transfers between devices, spread(): lax.all_to_all(jnp.broadcast_to(block[None], (size,) + block.shape), axis...  22.8 us
    all_to_all x1, blocking collectives, spread(): lax.all_to_all(jnp.broadcast_to(block[None], (size,) + block.shape), axis...  22.3 us
    all_to_all x1, waiting for transfers between devices, shards(): lax.all_to_all(partial.reshape(mp, shard_rows, features), 'mp', 0, 0)  14.1 us
  transfers between devices with their start and end apart: 12, of which 9 were waited for; matrix products, arithmetic and copies ran while one was open for 5% of the time, Pallas kernels for 0%

commit v1 on v0

--- a/solution.py
+++ b/solution.py
@@ -149,7 +149,9 @@
     token_ids = utterance_ids(mine(token_lengths)[0], tokens.shape[0])
     out_sent = lax.ppermute(own[3, :, half:], "segment", [(0, 1)])
     out_part = jnp.where(first, own[3, :, :half], out_sent)
-    out_part = lax.all_gather(out_part, "mp", axis=0, tiled=True)
+    out_part = jnp.concatenate(
+        lax.all_to_all(jnp.stack([out_part] * lax.axis_size("mp")), "mp", 0, 0), axis=0
+    )
     out_rest = swap(out_part)
     enc_full = spread(inputs, "mp").reshape(rows, features)
     other = swap(own)

time: 380 us -> 388 us (1.021)
    all_to_all x0 -> x1, waiting for transfers between devices: none -> 29.5 us  [shards(): lax.all_to_all(jnp.stack([out_part] * lax.axis_size('mp')), 'mp', 0, 0)]
    all_gather x1 -> x0, waiting for transfers between devices: 23.2 us -> none  [shards(): out_part = lax.all_gather(out_part, 'mp', axis=0, tiled=True)]
    ppermute x5, starting transfers between devices: 23.9 us -> 19 us  [swap(): return lax.ppermute(block, 'segment', [(0, 1), (1, 0)])]
  transfers between devices with their start and end apart: 12 -> 12, of which waited for: 9 -> 9; matrix products, arithmetic and copies ran while one was open for 5% -> 7% of each run, Pallas kernels for 0% -> 0%
where the time goes in v1:
time: 388 us; the launch traced here: 386 us
  waiting for transfers between devices  223 us (57%)
  starting transfers between devices  50 us (13%)
  blocking collectives  45.9 us (12%)
  matrix products  26.6 us (7%)
  other arithmetic  15.5 us (4%)
  between operations  14 us (4%)
  local copies, waits for them, and re-layouts  11.6 us (3%)
    psum x1, waiting for transfers between devices, shards(): dec_total = lax.psum(dec_part, 'dp')  140 us
    all_to_all x3, waiting for transfers between devices, spread(): lax.all_to_all(jnp.broadcast_to(block[None], (size,) + block.shape), axis...  35.2 us
    all_to_all x1, waiting for transfers between devices, shards(): lax.all_to_all(jnp.stack([out_part] * lax.axis_size('mp')), 'mp', 0, 0)  29.5 us
    all_to_all x1, blocking collectives, share_sum(): lax.all_to_all(blocks, axis, 0, 0).astype(jnp.float32)  23.6 us
    all_to_all x3, starting transfers between devices, spread(): lax.all_to_all(jnp.broadcast_to(block[None], (size,) + block.shape), axis...  22.5 us
    all_to_all x1, blocking collectives, spread(): lax.all_to_all(jnp.broadcast_to(block[None], (size,) + block.shape), axis...  22.3 us
    ppermute x5, starting transfers between devices, swap(): return lax.ppermute(block, 'segment', [(0, 1), (1, 0)])  19 us
    all_to_all x1, waiting for transfers between devices, shards(): lax.all_to_all(partial.reshape(mp, shard_rows, features), 'mp', 0, 0)  14.2 us
  transfers between devices with their start and end apart: 12, of which 9 were waited for; matrix products, arithmetic and copies ran while one was open for 7% of the time, Pallas kernels for 0%

profile of v1, /device:TPU:1, one launch (start us, length us, event | category | flops | bytes accessed | tf_op | source)
XLA Modules:
  0.0 386.4 jit_solution(17197426798169045118)
XLA Ops:
  8.4 10.9 %all-to-all-start = ((bf16[8,32,1280]{2,1,0:T(8,128)(2,1)}), bf16[8,32,1280]{2,1,0:T(8,128)(2,1)S(1)}, u32[]{:S(2)}, u32[]{:S(2)}) async-start(bf16[8,32,1280]{2,1,0:T(8,128)(2,1)} %broadcast_in_dim.31), calls=%async_computation | async-start | bytes 1310720 | tf_op jit(solution)/shard_map/all_to_all | solution.py:104
  19.3 2.9 collective-permute-start
  28.3 11.7 %all-to-all-done = bf16[8,32,1280]{2,1,0:T(8,128)(2,1)S(1)} async-done(((bf16[8,32,1280]{2,1,0:T(8,128)(2,1)}), bf16[8,32,1280]{2,1,0:T(8,128)(2,1)S(1)}, u32[]{:S(2)}, u32[]{:S(2)}) %all-to-all-start) | async-done | bytes 655392 | tf_op jit(solution)/shard_map/all_to_all | solution.py:104
  41.2 3.6 all-to-all-start.2
  45.6 2.9 broadcast_select_fusion.1
  50.0 29.5 %all-to-all-done.2 = bf16[8,128,640]{2,1,0:T(8,128)(2,1)S(1)} async-done(((bf16[8,128,640]{2,1,0:T(8,128)(2,1)}), bf16[8,128,640]{2,1,0:T(8,128)(2,1)S(1)}, u32[]{:S(2)}, u32[]{:S(2)}) %all-to-all-start.2) | async-done | bytes 1310752 | tf_op jit(solution)/shard_map/all_to_all | solution.py:153
  79.5 2.4 collective-permute-start.2
  84.6 3.5 all-to-all-start.1
  89.4 1.9 convolution_convert_fusion.11
  91.3 1.4 copy.38
  92.7 1.8 convolution_convert_fusion.10
  94.5 1.4 copy.39
  96.0 10.2 %all-to-all-done.1 = bf16[8,256,128]{2,1,0:T(8,128)(2,1)S(1)} async-done(((bf16[8,256,128]{2,1,0:T(8,128)(2,1)}), bf16[8,256,128]{2,1,0:T(8,128)(2,1)S(1)}, u32[]{:S(2)}, u32[]{:S(2)}) %all-to-all-start.1) | async-done | bytes 524320 | tf_op jit(solution)/shard_map/all_to_all | solution.py:104
  107.1 2.2 fusion.73
  114.1 2.4 fusion.25
  121.4 2.2 fusion.2
  123.6 3.5 all-to-all-start.3
  127.1 1.6 pad_maximum_fusion
  128.9 2.3 collective-permute-start.3
  133.7 14.2 %all-to-all-done.3 = bf16[8,32,1280]{2,1,0:T(8,128)(2,1)S(1)} async-done(((bf16[8,32,1280]{2,1,0:T(8,128)(2,1)}), bf16[8,32,1280]{2,1,0:T(8,128)(2,1)S(1)}, u32[]{:S(2)}, u32[]{:S(2)}) %all-to-all-start.3) | async-done | bytes 655392 | tf_op jit(solution)/shard_map/all_to_all | solution.py:212
  148.3 22.3 %all_to_all.35 = bf16[8,32,1280]{2,1,0:T(8,128)(2,1)S(1)} all-to-all(bf16[8,32,1280]{2,1,0:T(8,128)(2,1)S(1)} %broadcast_in_dim.37), channel_id=1, replica_groups=mesh['dp'=32,'segment'=2,'mp'=8] {'mp'}, dimensions={0} | all-to-all | bytes 1310720 | tf_op jit(solution)/shard_map/all_to_all | solution.py:104
  172.3 1.5 convolution_convert_fusion.7
  174.1 1.4 fusion.16
  176.3 3.2 collective-permute-start.4
  179.5 1.5 collective-permute-done.4
  181.2 23.6 %all_to_all.36 = bf16[32,8,8,128]{3,2,1,0:T(8,128)(2,1)S(1)} all-to-all(bf16[32,8,8,128]{3,2,1,0:T(8,128)(2,1)S(1)} %bitcast.182), channel_id=1, replica_groups=mesh['dp'=32,'segment'=2,'mp'=8] {'dp'}, dimensions={0} | all-to-all | bytes 1048576 | tf_op jit(solution)/shard_map/all_to_all | solution.py:108
  205.8 8.1 %all-to-all-start.6 = ((bf16[32,8,8,128]{3,2,1,0:T(8,128)(2,1)}), bf16[32,8,8,128]{3,2,1,0:T(8,128)(2,1)S(1)}, u32[]{:S(2)}, u32[]{:S(2)}) async-start(bf16[32,8,8,128]{3,2,1,0:T(8,128)(2,1)} %broadcast_in_dim.42), calls=%async_computation.6 | async-start | bytes 1048576 | tf_op jit(solution)/shard_map/all_to_all | solution.py:104
  214.7 13.3 %all-to-all-done.6 = bf16[32,8,8,128]{3,2,1,0:T(8,128)(2,1)S(1)} async-done(((bf16[32,8,8,128]{3,2,1,0:T(8,128)(2,1)}), bf16[32,8,8,128]{3,2,1,0:T(8,128)(2,1)S(1)}, u32[]{:S(2)}, u32[]{:S(2)}) %all-to-all-start.6) | async-done | bytes 524320 | tf_op jit(solution)/shard_map/all_to_all | solution.py:104
  228.1 140.2 %all-reduce.3.cloned.1.call-done = bf16[384,640]{1,0:T(8,128)(2,1)} async-done(((bf16[384,640]{1,0:T(8,128)(2,1)}), bf16[384,640]{1,0:T(8,128)(2,1)}) %all-reduce.3.cloned.1.call-update) | async-done | bytes 491536 | tf_op jit(solution)/shard_map/psum | solution.py:214
  368.3 8.2 %collective-permute-start.5 = (bf16[384,640]{1,0:T(8,128)(2,1)S(1)}, bf16[384,640]{1,0:T(8,128)(2,1)S(1)}, u32[]{:S(2)}, u32[]{:S(2)}) collective-permute-start(bf16[384,640]{1,0:T(8,128)(2,1)S(1)} %broadcast_select_fusion.4), channel_id=1, source_target_pairs={{0,8},{8,0},{1,9},{9,1},{2,10},{10,2},{3,11},{11,3},{4,12},{12,4},... | collective-permute-start | bytes 1474568 | tf_op jit(solution)/shard_map/ppermute | solution.py:112
  376.6 1.5 collective-permute-done.5
  378.1 1.4 maximum_convert_fusion
  (142 shorter events, 33.7 us)
Async XLA Ops:
  6.5 86.2 %copy-start = (bf16[2,64,1280]{2,1,0:T(8,128)(2,1)S(1)}, bf16[2,64,1280]{2,1,0:T(8,128)(2,1)}, u32[]{:S(2)}) copy-start(bf16[2,64,1280]{2,1,0:T(8,128)(2,1)} %param.10) | copy-start | bytes 983044
  6.5 17.8 %copy-start.19 = (s32[2,1,4]{2,1,0:T(1,128)S(1)}, s32[2,1,4]{2,1,0:T(1,128)}, u32[]{:S(2)}) copy-start(s32[2,1,4]{2,1,0:T(1,128)} %param.11) | copy-start | bytes 100
  6.5 17.8 %copy-start.20 = (s32[2,1,4]{2,1,0:T(1,128)S(1)}, s32[2,1,4]{2,1,0:T(1,128)}, u32[]{:S(2)}) copy-start(s32[2,1,4]{2,1,0:T(1,128)} %param.12) | copy-start | bytes 100
  6.5 18.1 %copy-start.7 = (bf16[2,64,1280]{2,1,0:T(8,128)(2,1)S(1)}, bf16[2,64,1280]{2,1,0:T(8,128)(2,1)}, u32[]{:S(2)}) copy-start(bf16[2,64,1280]{2,1,0:T(8,128)(2,1)} %param.9) | copy-start | bytes 983044
  7.5 19.2 %copy-start.13 = (f32[3,1280]{1,0:T(4,128)S(1)}, f32[3,1280]{1,0:T(4,128)}, u32[]{:S(2)}) copy-start(f32[3,1280]{1,0:T(4,128)} %param.15) | copy-start | bytes 46084
  7.5 19.2 %copy-start.14 = (f32[3,1280]{1,0:T(4,128)S(1)}, f32[3,1280]{1,0:T(4,128)}, u32[]{:S(2)}) copy-start(f32[3,1280]{1,0:T(4,128)} %param.14) | copy-start | bytes 46084
  8.4 31.6 %all-to-all-start = ((bf16[8,32,1280]{2,1,0:T(8,128)(2,1)}), bf16[8,32,1280]{2,1,0:T(8,128)(2,1)S(1)}, u32[]{:S(2)}, u32[]{:S(2)}) async-start(bf16[8,32,1280]{2,1,0:T(8,128)(2,1)} %broadcast_in_dim.31), calls=%async_computation | async-start | bytes 1310720 | tf_op jit(solution)/shard_map/all_to_all | solution.py:104
  19.3 26.4 %collective-permute-start = (bf16[4,128,1280]{2,1,0:T(8,128)(2,1)}, bf16[4,128,1280]{2,1,0:T(8,128)(2,1)}, u32[]{:S(2)}, u32[]{:S(2)}) collective-permute-start(bf16[4,128,1280]{2,1,0:T(8,128)(2,1)} %bitcast.2), channel_id=1, source_target_pairs={{0,8},{8,0},{1,9},{9,1},{2,10},{10,2},{3,11},{11,3},{4,12},{12,4},... | collective-permute-start | bytes 3932168 | tf_op jit(solution)/shard_map/ppermute | solution.py:112
  23.1 4.3 %collective-permute-start.1 = (bf16[128,640]{1,0:T(8,128)(2,1)S(1)}, bf16[128,640]{1,0:T(8,128)(2,1)S(1)}, u32[]{:S(2)}, u32[]{:S(2)}) collective-permute-start(bf16[128,640]{1,0:T(8,128)(2,1)S(1)} %slice_bitcast_fusion.18), channel_id=1, source_target_pairs={{0,8},{1,9},{2,10},{3,11},{4,12},{5,13},{6,14},{7,15},{16,24},{17,... | collective-permute-start | bytes 491528 | tf_op jit(solution)/shard_map/ppermute | solution.py:150
  24.8 1.9 copy-start.17
  26.1 57.0 %copy-start.9 = (pred[256,256]{0,1:T(8,128)(4,1)}, pred[256,256]{0,1:T(8,128)(4,1)S(1)}, u32[]{:S(2)}) copy-start(pred[256,256]{0,1:T(8,128)(4,1)S(1)} %broadcast_compare_fusion) | copy-start | bytes 196612
  41.2 38.3 %all-to-all-start.2 = ((bf16[8,128,640]{2,1,0:T(8,128)(2,1)}), bf16[8,128,640]{2,1,0:T(8,128)(2,1)S(1)}, u32[]{:S(2)}, u32[]{:S(2)}) async-start(bf16[8,128,640]{2,1,0:T(8,128)(2,1)} %stack.2), calls=%async_computation.2 | async-start | bytes 2621440 | tf_op jit(solution)/shard_map/all_to_all | solution.py:153
  48.9 34.1 %copy-start.21 = (bf16[256,128]{0,1:T(8,128)(2,1)}, bf16[256,128]{0,1:T(8,128)(2,1)S(1)}, u32[]{:S(2)}) copy-start(bf16[256,128]{0,1:T(8,128)(2,1)S(1)} %convolution_convert_fusion.5) | copy-start | bytes 196612
  49.6 34.0 %copy-start.23 = (bf16[256,128]{0,1:T(8,128)(2,1)}, bf16[256,128]{0,1:T(8,128)(2,1)S(1)}, u32[]{:S(2)}) copy-start(bf16[256,128]{0,1:T(8,128)(2,1)S(1)} %convolution_convert_fusion.6) | copy-start | bytes 196612
  50.0 33.6 %copy-start.25 = (bf16[256,128]{0,1:T(8,128)(2,1)}, bf16[256,128]{0,1:T(8,128)(2,1)S(1)}, u32[]{:S(2)}) copy-start(bf16[256,128]{0,1:T(8,128)(2,1)S(1)} %convolution_convert_fusion.4) | copy-start | bytes 196612
  79.5 4.1 %copy-start.1 = (bf16[8,128,640]{2,1,0:T(8,128)(2,1)}, bf16[8,128,640]{2,1,0:T(8,128)(2,1)S(1)}, u32[]{:S(2)}) copy-start(bf16[8,128,640]{2,1,0:T(8,128)(2,1)S(1)} %all-to-all-done.2) | copy-start | bytes 3932164
  79.5 27.6 %collective-permute-start.2 = (bf16[1024,640]{1,0:T(8,128)(2,1)S(1)}, bf16[1024,640]{1,0:T(8,128)(2,1)}, u32[]{:S(2)}, u32[]{:S(2)}) collective-permute-start(bf16[1024,640]{1,0:T(8,128)(2,1)S(1)} %bitcast.175), channel_id=1, source_target_pairs={{0,8},{8,0},{1,9},{9,1},{2,10},{10,2},{3,11},{11,3},{4,12},{12,4},... | collective-permute-start | bytes 3932168 | tf_op jit(solution)/shard_map/ppermute | solution.py:112
  83.1 1.6 copy-start.29
  84.6 21.5 %all-to-all-start.1 = ((bf16[8,256,128]{2,1,0:T(8,128)(2,1)}), bf16[8,256,128]{2,1,0:T(8,128)(2,1)S(1)}, u32[]{:S(2)}, u32[]{:S(2)}) async-start(bf16[8,256,128]{2,1,0:T(8,128)(2,1)} %broadcast_in_dim.34), calls=%async_computation.1 | async-start | bytes 1048576 | tf_op jit(solution)/shard_map/all_to_all | solution.py:104
  107.1 2.2 copy-start.2
  110.8 1.8 copy-start.11
  119.2 2.2 copy-start.3
  123.6 24.2 %all-to-all-start.3 = ((bf16[8,32,1280]{2,1,0:T(8,128)(2,1)}), bf16[8,32,1280]{2,1,0:T(8,128)(2,1)S(1)}, u32[]{:S(2)}, u32[]{:S(2)}) async-start(bf16[8,32,1280]{2,1,0:T(8,128)(2,1)} %bitcast.38), calls=%async_computation.3 | async-start | bytes 1310720 | tf_op jit(solution)/shard_map/all_to_all | solution.py:212
  128.9 3.8 collective-permute-start.3
  170.6 1.7 copy-start.22
  170.6 1.7 copy-start.24
  170.6 1.7 copy-start.30
  176.3 4.7 %collective-permute-start.4 = (bf16[384,640]{1,0:T(8,128)(2,1)S(1)}, bf16[384,640]{1,0:T(8,128)(2,1)S(1)}, u32[]{:S(2)}, u32[]{:S(2)}) collective-permute-start(bf16[384,640]{1,0:T(8,128)(2,1)S(1)} %select_convert_fusion), channel_id=1, source_target_pairs={{0,8},{8,0},{1,9},{9,1},{2,10},{10,2},{3,11},{11,3},{4,12},{12,4},... | collective-permute-start | bytes 1474568 | tf_op jit(solution)/shard_map/ppermute | solution.py:112
  205.8 22.2 %all-to-all-start.6 = ((bf16[32,8,8,128]{3,2,1,0:T(8,128)(2,1)}), bf16[32,8,8,128]{3,2,1,0:T(8,128)(2,1)S(1)}, u32[]{:S(2)}, u32[]{:S(2)}) async-start(bf16[32,8,8,128]{3,2,1,0:T(8,128)(2,1)} %broadcast_in_dim.42), calls=%async_computation.6 | async-start | bytes 1048576 | tf_op jit(solution)/shard_map/all_to_all | solution.py:104
  214.0 154.3 %all-reduce.3.cloned.1.call-start = ((), (), s32[]{:S(2)}) async-start(), calls=%async_computation.7 | async-start | bytes 983040 | tf_op jit(solution)/shard_map/psum | solution.py:214
  368.3 9.8 %copy-start.5 = (bf16[384,640]{1,0:T(8,128)(2,1)S(1)}, bf16[384,640]{1,0:T(8,128)(2,1)}, u32[]{:S(2)}) copy-start(bf16[384,640]{1,0:T(8,128)(2,1)} %all-reduce.3.cloned.1.call-done) | copy-start | bytes 1474564
  368.3 9.7 %collective-permute-start.5 = (bf16[384,640]{1,0:T(8,128)(2,1)S(1)}, bf16[384,640]{1,0:T(8,128)(2,1)S(1)}, u32[]{:S(2)}, u32[]{:S(2)}) collective-permute-start(bf16[384,640]{1,0:T(8,128)(2,1)S(1)} %broadcast_select_fusion.4), channel_id=1, source_target_pairs={{0,8},{8,0},{1,9},{9,1},{2,10},{10,2},{3,11},{11,3},{4,12},{12,4},... | collective-permute-start | bytes 1474568 | tf_op jit(solution)/shard_map/ppermute | solution.py:112
  (11 other events, 14.4 us)
Sparse Core Ops, SparseCore 0:
  218.2 150.0 all-reduce.2
